TPU v7x, 128 devices: a whole 4x4x4 slice. The times are simulated.
128 devices in a mesh: sensor: 16 (over y, z_lo, core), channel: 4 (over x), tm: 2 (over z_hi).
Axes of the slice: x: 4, y: 4, z: 4 (z_hi: 2, z_lo: 2; z = z_hi * 2 + z_lo), core: 2. Of those that a mesh axis runs over, the one named last changes fastest.
Arguments:
- tensor: float32 [12288, 128, 512], P('sensor', 'tm', 'channel'), may hold values from -6 to 6
- core: float32 [64, 64, 32], replicated, may hold values from -0.015625 to 0.015625
- sensor_factor: float32 [12288, 64], P('sensor'), may hold values from -6 to 6
- channel_factor: float32 [512, 64], P('channel'), may hold values from -6 to 6
- time_factor: float32 [128, 32], P('tm'), may hold values from -6 to 6
- neighbour_ids: int32 [96, 4], P('sensor'), may hold values from 0 to 95
- edge_weights: int32 [96, 4, 128, 128], P('sensor'), may hold values from 0 to 3
Outputs:
- core_grad: float32 [64, 64, 32], replicated
- sensor_grad: float32 [12288, 64], P(('sensor', 'channel', 'tm'))
- channel_grad: float32 [512, 64], P('channel')
- time_grad: float32 [128, 32], P('tm')
All inputs are finite; a program needn't handle non-finite values.
Results may differ from a plain program's by a relative error of at most 0.0001.
Values sent between devices are 32-bit elements; how exact they have to be, the bound alone decides.
A program may use at most 192 MiB of HBM per device.

v0:
```python
import math

import jax
import jax.numpy as jnp
from jax import lax
from jax.sharding import PartitionSpec as P

lap_weight = 1.0 / 512.0
highest = lax.Precision.HIGHEST


def pulled_rows(whole_factor, neighbour_ids, weights_float, block):
    whole = whole_factor.reshape(-1, block, whole_factor.shape[-1])
    neighbours = whole[neighbour_ids]
    return jnp.einsum("bnic,bncd->bid", weights_float, neighbours, precision=highest)


def on_device(
    tensor, core, sensor_factor, channel_factor, time_factor, neighbour_ids, edge_weights
):
    sensor_rows, time_rows, chan_rows = tensor.shape
    rank_one, rank_two, rank_three = core.shape
    n_sensor = lax.axis_size("sensor")
    n_channel = lax.axis_size("channel")
    n_time = lax.axis_size("tm")
    total_sensors = sensor_rows * n_sensor
    total_time = time_rows * n_time
    total_chan = chan_rows * n_channel
    core_time = jnp.einsum("rst,kt->rks", core, time_factor, precision=highest)
    core_both = jnp.einsum("rks,js->rkj", core_time, channel_factor, precision=highest)
    core_chan = jnp.einsum("rst,js->rtj", core, channel_factor, precision=highest)
    flat_core = core_both.reshape(rank_one, time_rows * chan_rows)
    residual = jnp.dot(sensor_factor, flat_core, precision=highest) - tensor.reshape(
        sensor_rows, time_rows * chan_rows
    )
    folded = jnp.dot(sensor_factor.T, residual, precision=highest)
    fit_part = jnp.dot(residual, flat_core.T, precision=highest) / math.sqrt(
        total_time * total_chan
    )
    folded3 = folded.reshape(rank_one, time_rows, chan_rows)
    inner = jnp.einsum("rkj,js->rks", folded3, channel_factor, precision=highest)
    core_part = jnp.einsum("rks,kt->rst", inner, time_factor, precision=highest) / math.sqrt(
        total_sensors * total_time * total_chan
    )
    chan_part = jnp.einsum("rkj,rks->js", folded3, core_time, precision=highest) / math.sqrt(
        total_sensors * total_time
    )
    time_part = jnp.einsum("rkj,rtj->kt", folded3, core_chan, precision=highest) / math.sqrt(
        total_sensors * total_chan
    )
    groups = n_channel * n_time
    share_index = lax.axis_index("channel") * n_time + lax.axis_index("tm")
    share = sensor_rows // groups
    block = edge_weights.shape[-1]
    weights_float = edge_weights.astype(jnp.float32)
    degree = jnp.sum(weights_float, axis=(1, 3)).reshape(sensor_rows)
    reduced = lax.psum_scatter(fit_part, ("channel", "tm"), scatter_dimension=0, tiled=True)
    whole_rows = lax.all_gather(sensor_factor, "sensor", axis=0, tiled=True)
    pulled = pulled_rows(whole_rows, neighbour_ids, weights_float, block).reshape(
        sensor_rows, rank_one
    )
    graph_all = lap_weight * (degree[:, None] * sensor_factor - pulled)
    graph_share = lax.dynamic_slice_in_dim(graph_all, share_index * share, share, 0)
    sensor_grad = reduced + graph_share
    core_grad = lax.psum(core_part, ("sensor", "channel", "tm"))
    channel_grad = lax.psum(chan_part, ("sensor", "tm"))
    time_grad = lax.psum(time_part, ("sensor", "channel"))
    return (core_grad, sensor_grad, channel_grad, time_grad)


def solution(mesh):
    return jax.shard_map(
        on_device,
        mesh=mesh,
        in_specs=(
            P("sensor", "tm", "channel"),
            P(),
            P("sensor", None),
            P("channel", None),
            P("tm", None),
            P("sensor", None),
            P("sensor", None, None, None),
        ),
        out_specs=(P(), P(("sensor", "channel", "tm"), None), P("channel", None), P("tm", None)),
        check_vma=False,
    )
```

profile of v0, /device:TPU:1, one launch (start us, length us, event | category | flops | bytes accessed | tf_op | source)
XLA Modules:
  0.0 551.3 jit_solution(13374377818562630704)
XLA Ops:
  8.0 0.0 copy-start
  8.0 0.0 copy-start.6
  8.0 0.0 reduce-scatter.4.cloned.1.call-start
  8.1 24.9 %copy.27 = f32[768,64,128]{0,2,1:T(8,128)} copy(f32[768,64,128]{2,1,0:T(8,128)} %param.7) | data formatting | bytes 50331648 | tf_op args[0]
  33.0 0.0 copy-done
  33.0 0.0 copy-done.6
  33.0 0.0 copy-start.5
  33.0 1.8 fusion.32
  34.8 0.0 copy-done.5
  34.8 0.0 copy-start.1
  34.8 0.0 copy-start.3
  34.8 1.8 fusion.5
  36.7 0.0 copy-done.1
  36.7 0.0 copy-done.3
  36.7 26.3 %bitcast_subtract_fusion = f32[768,8192]{0,1:T(8,128)} fusion(f32[768,64,128]{0,2,1:T(8,128)} %copy.27, f32[768,64]{0,1:T(8,128)S(1)} %copy-done.3, f32[8,8,64,128]{3,2,1,0:T(8,128)S(1)} %bitcast.77), kind=kOutput, calls=%fused_computation.1 | convolution fusion | flops 4838129664 | bytes 52625408 | tf_op jit(solution)/shard_map/dot_general | solution.py:33
  63.0 0.0 copy-start.4
  63.0 20.9 %fusion.14 = f32[768,64]{0,1:T(8,128)S(1)} fusion(f32[768,8192]{0,1:T(8,128)} %bitcast_subtract_fusion, f32[8,8,64,128]{3,2,1,0:T(8,128)S(1)} %bitcast.78), kind=kOutput, calls=%fused_computation.18 | convolution fusion | flops 4831887360 | bytes 27459584 | tf_op jit(solution)/shard_map/dot_general | solution.py:37
  83.8 0.9 copy.34
  84.8 0.0 reduce-scatter.4.cloned.1.call-update
  84.8 0.0 all-gather.2.cloned.1.call-start
  84.8 0.5 all-gather.2.cloned.1.call-update
  85.4 0.0 all-reduce.2.cloned.1.call-start
  85.4 0.0 copy-done.4
  85.4 27.7 %convolution_bitcast_fusion = f32[8,8,64,128]{3,1,2,0:T(8,128)S(1)} fusion(f32[768,8192]{0,1:T(8,128)} %bitcast_subtract_fusion, f32[768,64]{0,1:T(8,128)S(1)} %copy-done.4), kind=kOutput, calls=%fused_computation.12 | convolution fusion | flops 4831838208 | bytes 27459584 | tf_op jit(solution)/shard_map/dot_general | solution.py:36
  113.2 0.4 copy.39
  113.5 1.9 fusion.28
  115.4 2.2 convolution_multiply_fusion
  117.6 0.0 all-reduce.2.cloned.1.call-update
  117.6 5.2 fusion.20
  122.9 0.0 copy-start.7
  122.9 1.9 fusion.26
  124.8 0.0 copy-done.7
  124.8 0.1 copy.28
  124.9 0.1 reshape.31
  125.0 1.6 convert_reduce_fusion
  126.6 129.5 %psum.22 = f32[128,64]{0,1:T(8,128)} all-reduce(f32[128,64]{0,1:T(8,128)S(1)} %fusion.20), channel_id=1, replica_groups=mesh['sensor'=16,'channel'=4,'tm'=2] {'sensor','tm'}, use_global_device_ids=true, to_apply=%region_3.0 | all-reduce | flops 8192 | bytes 65536 | tf_op jit(solution)/shard_map/psum | solution.py:66
  256.1 3.0 fusion.23
  259.1 271.6 %psum.23 = f32[64,32]{0,1:T(8,128)} all-reduce(f32[64,32]{0,1:T(8,128)S(1)} %fusion.23), channel_id=1, replica_groups=mesh['sensor'=16,'channel'=4,'tm'=2] {'sensor','channel'}, use_global_device_ids=true, to_apply=%region_4.0 | all-reduce | flops 2048 | bytes 16384 | tf_op jit(solution)/shard_map/psum | solution.py:67
  530.7 0.1 dynamic-slice
  530.7 0.0 reduce-scatter.4.cloned.1.call-done
  530.8 0.9 copy.35
  531.6 0.0 all-gather.2.cloned.1.call-done
  531.7 4.0 copy_bitcast_fusion
  535.6 0.0 copy-start.2
  535.6 2.6 gather_fusion
  538.2 0.0 copy-done.2
  538.2 1.8 fusion.11
  540.1 1.6 fusion.25
  541.6 0.0 all-reduce.2.cloned.1.call-done
  541.6 2.3 copy.54
  (3 shorter events, 0.0 us)
Async XLA Ops:
  8.0 25.0 %copy-start = (f32[64,64,32]{1,2,0:T(8,128)S(1)}, f32[64,64,32]{1,2,0:T(8,128)}, u32[]{:S(2)}) copy-start(f32[64,64,32]{1,2,0:T(8,128)} %param.8) | copy-start | bytes 1572868
  8.0 24.9 %copy-start.6 = (f32[64,32]{0,1:T(8,128)S(1)}, f32[64,32]{0,1:T(8,128)}, u32[]{:S(2)}) copy-start(f32[64,32]{0,1:T(8,128)} %param.11) | copy-start | bytes 24580
  8.0 522.7 %reduce-scatter.4.cloned.1.call-start = ((), (), s32[]{:S(2)}) async-start(), calls=%async_computation.3 | async-start | bytes 442368
  33.0 1.9 copy-start.5
  34.8 1.9 copy-start.1
  34.8 1.9 copy-start.3
  63.0 22.5 %copy-start.4 = (f32[768,64]{0,1:T(8,128)S(1)}, f32[768,64]{0,1:T(8,128)}, u32[]{:S(2)}) copy-start(f32[768,64]{0,1:T(8,128)} %param.9) | copy-start | bytes 589828
  84.8 446.9 %all-gather.2.cloned.1.call-start = ((), (), s32[]{:S(2)}) async-start(), calls=%async_computation.2 | async-start | bytes 3342336 | tf_op jit(solution)/shard_map/all_gather | solution.py:58
  85.4 456.2 %all-reduce.2.cloned.1.call-start = ((), (), s32[]{:S(2)}) async-start(), calls=%async_computation.1 | async-start | bytes 2097152 | tf_op jit(solution)/shard_map/psum | solution.py:65
  122.9 1.9 copy-start.7
  535.6 2.6 copy-start.2
Sparse Core Ops, SparseCore 0:
  84.9 73.0 reduce-scatter.3
  163.4 148.4 all-reduce.1
Sparse Core Ops, SparseCore 1:
  87.0 39.4 all-gather.1
where the time goes:
time: 557 us; the launch traced here: 551 us
  blocking collectives  401 us (72%)
  matrix products  94.5 us (17%)
  local copies, waits for them, and re-layouts  36.2 us (6%)
  between operations  15.7 us (3%)
    psum x1, blocking collectives, on_device(): time_grad = lax.psum(time_part, ('sensor', 'channel'))  272 us
    psum x1, blocking collectives, on_device(): channel_grad = lax.psum(chan_part, ('sensor', 'tm'))  130 us
    unnamed x21, local copies, waits for them, and re-layouts  29.4 us
    dot_general x1, matrix products, on_device(): folded = jnp.dot(sensor_factor.T, residual, precision=highest)  27.7 us
    dot_general x1, matrix products, on_device(): jnp.dot(sensor_factor, flat_core, precision=highest)  26.3 us
    dot_general x1, matrix products, on_device(): jnp.dot(residual, flat_core.T, precision=highest)  20.9 us
  transfers between devices with their start and end apart: 3, of which 0 were waited for; matrix products, arithmetic and copies ran while one was open for 10% of the time, Pallas kernels for 0%

commit v1 on v0

v1 whole, which is shorter than its diff:
```python
import functools
import math

import jax
import jax.numpy as jnp
from jax import lax
from jax.experimental import pallas as pl
from jax.experimental.pallas import tpu as pltpu
from jax.sharding import PartitionSpec as P

lap_weight = 1.0 / 512.0
high = lax.Precision.HIGH
highest = lax.Precision.HIGHEST
f32 = jnp.float32
bf16 = jnp.bfloat16
AXES = ("sensor", "channel", "tm")


def split(value):
    top = value.astype(bf16)
    return top, (value - top.astype(f32)).astype(bf16)


def slab(steps, tensor_ref, rows_ref, chan_ref, ct_ref, folded_ref, fit_ref, fold_lhs, chan_lhs, square_lhs, fit_sum, gram):
    step = pl.program_id(0)
    sensors, slab_steps, chans = tensor_ref.shape
    rank = rows_ref.shape[0]

    @pl.when(step == 0)
    def _():
        rows = rows_ref[...]
        top, low = split(rows)
        fold_lhs[0:rank, 0:sensors] = top
        fold_lhs[0:rank, sensors:] = top
        fold_lhs[rank:, 0:sensors] = low
        fold_lhs[rank:, sensors:] = jnp.zeros_like(low)
        square = lax.dot_general(rows, rows, (((1,), (1,)), ((), ())), precision=highest, preferred_element_type=f32)
        top, low = split(square)
        square_lhs[...] = jnp.concatenate([top, top, low, jnp.zeros_like(low)], axis=1)
        top, low = split(chan_ref[...].T)
        chan_lhs[...] = jnp.concatenate([top, low, top], axis=1)
        fit_sum[...] = jnp.zeros_like(fit_sum)
        gram[...] = jnp.zeros_like(gram)

    flat = tensor_ref.reshape(sensors * slab_steps, chans)
    model = jnp.dot(chan_lhs[...], ct_ref[...], preferred_element_type=f32)
    lower_half = lax.broadcasted_iota(jnp.int32, (chans, 2 * rank), 1) < rank
    for pair in range(slab_steps // 2):
        wide, narrow = [], []
        for k in (2 * pair, 2 * pair + 1):
            piece = model[:, k * 2 * rank : (k + 1) * 2 * rank]
            top = piece.astype(bf16).astype(f32)
            wide.append(jnp.where(lower_half, top, piece - top).astype(bf16))
            narrow.append(jnp.where(lower_half, top, 0.0).astype(bf16))
        both = jnp.concatenate(wide, axis=0)
        first = jnp.concatenate(narrow, axis=0)
        data = jnp.concatenate(
            [flat[pl.ds(2 * pair, sensors, stride=slab_steps), :], flat[pl.ds(2 * pair + 1, sensors, stride=slab_steps), :]], axis=1
        )
        top, low = split(data)
        part = jnp.dot(fold_lhs[...], jnp.concatenate([top, low], axis=0), preferred_element_type=f32)
        own = lax.dot_general(
            square_lhs[...], jnp.concatenate([both, first], axis=1), (((1,), (1,)), ((), ())), preferred_element_type=f32
        )
        total = own - (part[:rank] + part[rank:])
        folded_ref[:, 2 * pair, :] = total[:, :chans]
        folded_ref[:, 2 * pair + 1, :] = total[:, chans:]
        fit_sum[...] += jnp.dot(
            jnp.concatenate([top, low], axis=1), jnp.concatenate([both, first], axis=0), preferred_element_type=f32
        )
        gram[...] += lax.dot_general(both, both, (((0,), (0,)), ((), ())), preferred_element_type=f32)

    @pl.when(step == steps - 1)
    def _():
        grams = gram[...]
        left = grams[:rank] + grams[rank:]
        square = left[:, :rank] + left[:, rank:]
        seen = fit_sum[...]
        model_fit = lax.dot_general(
            rows_ref[...], square, (((0,), (0,)), ((), ())), precision=highest, preferred_element_type=f32
        )
        fit_ref[...] = model_fit - (seen[:, :rank] + seen[:, rank:])


def big_pass(tensor, rows, chan, ct, slab_steps=8):
    sensors, times, chans = tensor.shape
    rank = rows.shape[0]
    rank_two = chan.shape[0]
    steps = times // slab_steps
    return pl.pallas_call(
        functools.partial(slab, steps),
        grid=(steps,),
        in_specs=[
            pl.BlockSpec((sensors, slab_steps, chans), lambda i: (0, i, 0)),
            pl.BlockSpec((rank, sensors), lambda i: (0, 0)),
            pl.BlockSpec((rank_two, chans), lambda i: (0, 0)),
            pl.BlockSpec((3 * rank_two, slab_steps * 2 * rank), lambda i: (0, i)),
        ],
        out_specs=[
            pl.BlockSpec((rank, slab_steps, chans), lambda i: (0, i, 0)),
            pl.BlockSpec((sensors, rank), lambda i: (0, 0)),
        ],
        out_shape=[jax.ShapeDtypeStruct((rank, times, chans), f32), jax.ShapeDtypeStruct((sensors, rank), f32)],
        scratch_shapes=[
            pltpu.VMEM((2 * rank, 2 * sensors), bf16),
            pltpu.VMEM((chans, 3 * rank_two), bf16),
            pltpu.VMEM((rank, 4 * rank), bf16),
            pltpu.VMEM((sensors, 2 * rank), f32),
            pltpu.VMEM((2 * rank, 2 * rank), f32),
        ],
        compiler_params=pltpu.CompilerParams(vmem_limit_bytes=50 * 2**20),
        cost_estimate=pl.CostEstimate(flops=8 * 10**9, bytes_accessed=32 * 2**20, transcendentals=0),
    )(tensor, rows, chan, ct)


def on_device(
    tensor, core, sensor_factor, channel_factor, time_factor, neighbour_ids, edge_weights
):
    sensor_rows, time_rows, chan_rows = tensor.shape
    rank_one, rank_two, rank_three = core.shape
    n_sensor = lax.axis_size("sensor")
    n_channel = lax.axis_size("channel")
    n_time = lax.axis_size("tm")
    total_sensors = sensor_rows * n_sensor
    total_time = time_rows * n_time
    total_chan = chan_rows * n_channel
    groups = n_channel * n_time
    chan_index = lax.axis_index("channel")
    time_index = lax.axis_index("tm")
    share_index = chan_index * n_time + time_index
    share = sensor_rows // groups
    block, slots = edge_weights.shape[-1], edge_weights.shape[1]
    blocks = edge_weights.shape[0]

    rows = sensor_factor.T
    block_rows = rows.reshape(rank_one, blocks, block).transpose(1, 0, 2)
    whole_rows = lax.all_gather(block_rows, "sensor", axis=0, tiled=True)

    core_time = jnp.einsum("rst,kt->skr", core, time_factor, precision=highest)
    twice = jnp.concatenate([core_time, core_time], axis=2).reshape(rank_two, time_rows * 2 * rank_one)
    top = lax.reduce_precision(twice, 8, 7)
    ct = jnp.concatenate([top, top, twice - top], axis=0).astype(bf16)
    folded3, fit = big_pass(tensor, rows, channel_factor.T, ct)

    pairs = blocks * slots // groups
    first = share_index * pairs
    weights = lax.dynamic_slice_in_dim(edge_weights.reshape(blocks * slots, block, block), first, pairs, 0).astype(f32)
    ids = lax.dynamic_slice_in_dim(neighbour_ids.reshape(blocks * slots), first, pairs, 0)
    near = jnp.stack([lax.dynamic_index_in_dim(whole_rows, ids[q], 0, keepdims=False) for q in range(pairs)])
    pulled = jnp.einsum("qac,qdc->qad", weights, near, precision=high)
    degree = jnp.sum(weights, axis=2)
    owner = (first + jnp.arange(pairs)) // slots
    chosen = (jnp.arange(blocks)[:, None] == owner[None, :]).astype(f32)
    degrees = jnp.sum(chosen[:, :, None] * degree[None], axis=1).reshape(sensor_rows)
    pulls = jnp.sum(chosen[:, :, None, None] * pulled[None], axis=1).reshape(sensor_rows, rank_one)
    fit_part = fit / math.sqrt(total_time * total_chan) + lap_weight * (degrees[:, None] * sensor_factor - pulls)
    sensor_grad = lax.psum_scatter(fit_part, ("channel", "tm"), scatter_dimension=0, tiled=True)

    inner = jnp.einsum("rkj,js->rks", folded3, channel_factor, precision=high)
    core_part = jnp.einsum("rks,kt->rts", inner, time_factor, precision=high)
    chan_part = jnp.einsum("rkj,skr->sj", folded3, core_time, precision=high)
    time_part = jnp.einsum("rks,rst->tk", inner, core, precision=high)
    chan_slots = jnp.where((jnp.arange(n_channel) == chan_index)[:, None, None], chan_part[None], 0.0)
    time_slots = jnp.where((jnp.arange(n_time) == time_index)[:, None, None], time_part[None], 0.0)
    packed = jnp.concatenate(
        [core_part.reshape(-1, 128), chan_slots.reshape(-1, 128), time_slots.reshape(-1, 128)], axis=0
    )
    total = lax.psum(packed, AXES)
    n_core = core_part.size // 128
    n_chan = n_channel * chan_part.size // 128
    core_grad = total[:n_core].reshape(rank_one, rank_three, rank_two).transpose(0, 2, 1)
    chan_all = total[n_core : n_core + n_chan].reshape(n_channel, rank_two, chan_rows)
    time_all = total[n_core + n_chan :].reshape(n_time, rank_three, time_rows)
    channel_grad = lax.dynamic_index_in_dim(chan_all, chan_index, 0, keepdims=False).T
    time_grad = lax.dynamic_index_in_dim(time_all, time_index, 0, keepdims=False).T
    return (
        core_grad / math.sqrt(total_sensors * total_time * total_chan),
        sensor_grad,
        channel_grad / math.sqrt(total_sensors * total_time),
        time_grad / math.sqrt(total_sensors * total_chan),
    )


def solution(mesh):
    return jax.shard_map(
        on_device,
        mesh=mesh,
        in_specs=(
            P("sensor", "tm", "channel"),
            P(),
            P("sensor", None),
            P("channel", None),
            P("tm", None),
            P("sensor", None),
            P("sensor", None, None, None),
        ),
        out_specs=(P(), P(("sensor", "channel", "tm"), None), P("channel", None), P("tm", None)),
        check_vma=False,
    )
```

time: 557 us -> 220 us (0.39)
  blocking collectives: 401 us -> 0 us
  waiting for transfers between devices: 0.58 us -> 137 us
  matrix products: 94.5 us -> 13.8 us
  local copies, waits for them, and re-layouts: 36.2 us -> 13.9 us
  Pallas kernels: 0 us -> 18.7 us
  other arithmetic: 3.17 us -> 13.7 us
  between operations: 15.7 us -> 21.5 us
    psum x2 -> x0, blocking collectives: 401 us -> none  [the longest x1 272 us: on_device(): time_grad = lax.psum(time_part, ('sensor', 'channel'))]
    psum x1, waiting for transfers between devices: 0.01 us -> 137 us  [on_device(): total = lax.psum(packed, AXES)]
    dot_general x11 -> x6, matrix products: 94.5 us -> 13.8 us  [the longest x1 3.96 us: on_device(): core_time = jnp.einsum('rst,kt->skr', core, time_factor, precision=highest)]
    unnamed x21, local copies, waits for them, and re-layouts: 29.4 us -> 2.12 us
    pallas_call x0 -> x1, Pallas kernels: none -> 18.7 us  [big_pass(): pl.pallas_call(functools.partial(slab, steps), grid=(steps,), in_specs=[p...]
    concatenate x0 -> x3, other arithmetic: none -> 7.78 us  [the longest x1 5 us: on_device(): jnp.concatenate([core_time, core_time], axis=2)]
  transfers between devices with their start and end apart: 3 -> 3, of which waited for: 0 -> 1; matrix products, arithmetic and copies ran while one was open for 10% -> 17% of each run, Pallas kernels for 0% -> 9%
where the time goes in v1:
time: 220 us; the launch traced here: 219 us
  waiting for transfers between devices  137 us (62%)
  between operations  21.5 us (10%)
  Pallas kernels  18.7 us (8%)
  local copies, waits for them, and re-layouts  13.9 us (6%)
  matrix products  13.8 us (6%)
  other arithmetic  13.7 us (6%)
    psum x1, waiting for transfers between devices, on_device(): total = lax.psum(packed, AXES)  137 us
    pallas_call x1, Pallas kernels, big_pass(): pl.pallas_call(functools.partial(slab, steps), grid=(steps,), in_specs=[p...  18.7 us
    concatenate x1, other arithmetic, on_device(): jnp.concatenate([core_time, core_time], axis=2)  5 us
    concatenate x1, local copies, waits for them, and re-layouts, on_device(): jnp.concatenate([core_time, core_time], axis=2)  4.51 us
  transfers between devices with their start and end apart: 3, of which 1 were waited for; matrix products, arithmetic and copies ran while one was open for 17% of the time, Pallas kernels for 9%

profile of v1, /device:TPU:1, one launch (start us, length us, event | category | flops | bytes accessed | tf_op | source)
XLA Modules:
  0.0 219.2 jit_solution(17743018920322256870)
XLA Ops:
  8.0 0.0 copy-start
  8.0 0.0 all-gather.2.cloned.1.call-start
  8.1 1.0 reshape.122
  9.1 0.7 copy.38
  9.8 0.0 all-gather.2.cloned.1.call-update
  9.8 0.0 all-reduce.2.cloned.1.call-start
  9.9 0.0 copy-done
  9.9 4.0 %convolution_bitcast_fusion = f32[64,64,64]{0,1,2:T(8,128)} fusion(f32[64,64,32]{1,2,0:T(8,128)S(1)} %copy-done, f32[64,32]{0,1:T(8,128)} %param.11), kind=kOutput, calls=%fused_computation.5 | convolution fusion | flops 100663296 | bytes 1581056 | tf_op jit(solution)/shard_map/rst,kt->skr/dot_general | solution.py:139
  13.8 5.0 %pad_maximum_fusion = f32[64,64,128]{0,1,2:T(8,128)} fusion(f32[64,64,64]{0,1,2:T(8,128)} %convolution_bitcast_fusion), kind=kLoop, calls=%fused_computation | loop fusion | flops 524288 | bytes 3145728 | tf_op jit(solution)/shard_map/concatenate | solution.py:140
  18.9 4.5 %copy.34 = f32[64,64,128]{2,1,0:T(8,128)S(1)} copy(f32[64,64,128]{0,1,2:T(8,128)} %pad_maximum_fusion) | data formatting | bytes 4194304 | tf_op jit(solution)/shard_map/concatenate | solution.py:140
  23.4 1.2 reduce-precision_convert_fusion
  24.6 0.0 copy-start.1
  24.6 0.0 copy-start.4
  24.6 1.9 pad_maximum_fusion.1.ct_ref
  26.5 0.0 copy-done.1
  26.5 0.0 copy-done.4
  26.5 18.7 %shard_map.102 = (f32[64,64,128]{2,1,0:T(8,128)S(1)}, f32[768,64]{1,0:T(8,128)S(1)}) custom-call(f32[768,64,128]{2,1,0:T(8,128)} %tensor_ref.1, f32[64,768]{1,0:T(8,128)S(1)} %bitcast.56, f32[64,128]{1,0:T(8,128)S(1)} %bitcast.57, bf16[192,8192]{1,0:T(8,128)(2,1)} %pad_maximum_fusion.1.ct_ref), custom_call_target="tpu_custom_call" | custom-call | flops 8000000000 | bytes 33554432 | tf_op jit(solution)/shard_map/pallas_call | solution.py:90
  45.3 0.0 copy-start.2
  45.3 1.0 fusion.11
  46.3 0.0 copy-done.2
  46.3 0.0 copy-start.5
  46.3 0.0 copy-start.7
  46.3 1.0 convolution_bitcast_fusion.3
  47.3 0.3 copy-done.5
  47.6 0.1 broadcast_select_fusion
  47.7 0.1 select_n.46
  47.7 0.1 broadcast_in_dim.56
  47.8 0.1 broadcast_in_dim.57
  47.9 0.0 copy-done.7
  47.9 3.2 %convolution_bitcast_fusion.1 = f32[64,32,64]{2,1,0:T(8,128)} fusion(f32[64,64,64]{2,1,0:T(8,128)} %copy-done.5, f32[64,32]{0,1:T(8,128)S(1)} %copy-done.7), kind=kOutput, calls=%fused_computation.6 | convolution fusion | flops 50331648 | bytes 1581056 | tf_op jit(solution)/shard_map/rks,kt->rts/dot_general | solution.py:160
  51.1 2.2 %reshape.120 = f32[1024,128]{1,0:T(8,128)} reshape(f32[64,32,64]{2,1,0:T(8,128)} %convolution_bitcast_fusion.1) | data formatting | bytes 1048576 | tf_op jit(solution)/shard_map/reshape | solution.py:166
  53.3 3.5 %convolution_bitcast_fusion.2 = f32[64,128]{1,0:T(8,128)S(1)} fusion(f32[64,64,64]{0,1,2:T(8,128)} %convolution_bitcast_fusion, f32[64,64,128]{2,1,0:T(8,128)S(1)} %get-tuple-element.6), kind=kOutput, calls=%fused_computation.7 | convolution fusion | flops 201326592 | bytes 3178496 | tf_op jit(solution)/shard_map/rkj,skr->sj/dot_general | solution.py:161
  56.8 0.0 copy-start.8
  56.8 0.1 bitcast_select_fusion
  56.9 0.0 copy-done.6
  57.0 0.0 copy-start.3
  57.0 0.9 pad_maximum_fusion.2
  57.9 0.0 all-reduce.2.cloned.1.call-update
  57.9 0.0 reduce-scatter.2.cloned.1.call-start
  57.9 0.0 copy-done.8
  57.9 0.1 copy.39
  58.0 0.1 reshape.123
  58.1 0.1 dynamic_slice.25
  58.2 0.6 fusion.18
  62.7 0.2 copy.37
  62.9 1.1 convert_reduce_fusion
  63.9 0.1 copy.36
  66.0 0.1 multiply_reduce_fusion.1
  66.1 0.8 constant_dynamic-slice_fusion.2
  66.9 1.2 fusion.3
  68.1 0.1 multiply_reduce_fusion
  68.2 0.2 copy.40
  68.4 0.0 copy-done.3
  68.4 0.9 fusion.2
  69.3 0.0 reduce-scatter.2.cloned.1.call-update
  69.4 137.3 %all-reduce.2.cloned.1.call-done = f32[1312,128]{1,0:T(8,128)} async-done(((f32[1312,128]{1,0:T(8,128)}), f32[1312,128]{1,0:T(8,128)}) %all-reduce.2.cloned.1.call-update) | async-done | bytes 671760 | tf_op jit(solution)/shard_map/psum | solution.py:168
  206.7 1.1 slice_multiply_fusion
  207.8 1.2 div.50
  209.0 0.0 slice-done
  209.0 0.1 reshape.126
  209.0 0.6 multiply_bitcast_fusion.1
  209.7 0.0 slice-done.1
  209.7 0.6 multiply_bitcast_fusion
  210.3 1.5 copy.41
  (9 shorter events, 0.0 us)
Async XLA Ops:
  8.0 1.9 copy-start
  8.0 58.1 %all-gather.2.cloned.1.call-start = ((), (), s32[]{:S(2)}) async-start(), calls=%async_computation.2 | async-start | bytes 3342336 | tf_op jit(solution)/shard_map/all_gather | solution.py:137
  9.8 196.8 %all-reduce.2.cloned.1.call-start = ((), (), s32[]{:S(2)}) async-start(), calls=%async_computation.1 | async-start | bytes 1343488 | tf_op jit(solution)/shard_map/psum | solution.py:168
  24.6 1.9 copy-start.1
  24.6 1.9 copy-start.4
  45.3 1.0 copy-start.2
  46.3 1.3 copy-start.5
  46.3 1.6 copy-start.7
  53.3 3.6 %copy-start.6 = (f32[1024,128]{1,0:T(8,128)S(1)}, f32[1024,128]{1,0:T(8,128)}, u32[]{:S(2)}) copy-start(f32[1024,128]{1,0:T(8,128)} %reshape.120) | copy-start | bytes 1572868
  56.8 1.1 copy-start.8
  57.0 11.4 %copy-start.3 = (f32[768,64]{1,0:T(8,128)S(1)}, f32[768,64]{1,0:T(8,128)}, u32[]{:S(2)}) copy-start(f32[768,64]{1,0:T(8,128)} %copy-done.2) | copy-start | bytes 589828
  57.9 152.4 %reduce-scatter.2.cloned.1.call-start = ((), (), s32[]{:S(2)}) async-start(), calls=%async_computation.3 | async-start | bytes 442368 | tf_op jit(solution)/shard_map/reduce_scatter | solution.py:157
  206.7 2.3 %slice-start = ((f32[1312,128]{1,0:T(8,128)}), f32[32,128]{1,0:T(8,128)S(1)}, s32[]{:S(2)}) async-start(f32[1312,128]{1,0:T(8,128)} %all-reduce.2.cloned.1.call-done), calls=%async_computation.4 | async-start | bytes 32768 | tf_op jit(solution)/shard_map/slice | solution.py:173
  206.7 3.0 %slice-start.1 = ((f32[1312,128]{1,0:T(8,128)}), f32[256,128]{1,0:T(8,128)S(1)}, s32[]{:S(2)}) async-start(f32[1312,128]{1,0:T(8,128)} %all-reduce.2.cloned.1.call-done), calls=%async_computation.5 | async-start | bytes 262144 | tf_op jit(solution)/shard_map/slice | solution.py:172
Sparse Core Ops, SparseCore 0:
  10.6 39.4 all-gather.1
  69.5 72.4 reduce-scatter.1
Sparse Core Ops, SparseCore 1:
  58.0 148.6 all-reduce.1

commit v2 on v1

--- a/solution.py
+++ b/solution.py
@@ -13,7 +13,6 @@
 highest = lax.Precision.HIGHEST
 f32 = jnp.float32
 bf16 = jnp.bfloat16
-AXES = ("sensor", "channel", "tm")
 
 
 def split(value):
@@ -111,6 +110,104 @@
         compiler_params=pltpu.CompilerParams(vmem_limit_bytes=50 * 2**20),
         cost_estimate=pl.CostEstimate(flops=8 * 10**9, bytes_accessed=32 * 2**20, transcendentals=0),
     )(tensor, rows, chan, ct)
+
+
+def place():
+    sensor = lax.axis_index("sensor")
+    return lax.axis_index("channel"), sensor // 4, lax.axis_index("tm") * 2 + lax.rem(sensor // 2, 2), lax.rem(sensor, 2)
+
+
+def device(x, y, z, core):
+    return ((y * 2 + lax.rem(z, 2)) * 2 + core, x, z // 2)
+
+
+def exchange(part_ref, fit_ref, total_ref, share_ref, half, from_core, from_x, quarter, from_y, piece, from_z, fit_x, fit_half, fit_z, sent, got):
+    x, y, z, core = place()
+    z_half = z // 2
+    turn = lambda value, d: lax.rem(value + d, 4)
+    x_peers = [(turn(x, d), y, z, core) for d in (1, 2, 3)]
+    y_peers = [(x, turn(y, d), z, core) for d in (1, 2, 3)]
+    z_peers = [(x, y, turn(z, d), core) for d in (1, 2, 3)]
+    core_peer = (x, y, z, 1 - core)
+    barrier = pltpu.get_barrier_semaphore()
+    for peer in [core_peer] + x_peers + y_peers + z_peers:
+        pl.semaphore_signal(barrier, inc=1, device_id=device(*peer), device_id_type=pl.DeviceIdType.MESH)
+    pl.semaphore_wait(barrier, 10)
+
+    slot = iter(range(21))
+
+    def send(source, target, peer):
+        at = next(slot)
+        copy = pltpu.make_async_remote_copy(
+            src_ref=source,
+            dst_ref=target,
+            send_sem=sent.at[at],
+            recv_sem=got.at[at],
+            device_id=device(*peer),
+            device_id_type=pl.DeviceIdType.MESH,
+        )
+        copy.start()
+        return copy
+
+    to_core = send(part_ref.at[1 - core], from_core, core_peer)
+    fits = [send(fit_ref.at[peer[0]], fit_x.at[d], peer) for d, peer in enumerate(x_peers)]
+    to_core.wait()
+    half[...] = part_ref[core] + from_core[...]
+    over_x = [send(half.at[peer[0]], from_x.at[d], peer) for d, peer in enumerate(x_peers)]
+    for copy in fits:
+        copy.wait()
+    fit_half[...] = (fit_ref[x] + fit_x[0]) + (fit_x[1] + fit_x[2])
+    fit_last = send(fit_half.at[1 - z_half], fit_z, z_peers[1])
+    for copy in over_x:
+        copy.wait()
+    quarter[...] = (half[x] + from_x[0]) + (from_x[1] + from_x[2])
+    over_y = [send(quarter.at[peer[1]], from_y.at[d], peer) for d, peer in enumerate(y_peers)]
+    fit_last.wait()
+    share_ref[...] = fit_half[z_half] + fit_z[...]
+    for copy in over_y:
+        copy.wait()
+    value = (quarter[y] + from_y[0]) + (from_y[1] + from_y[2])
+    piece[...] = value
+    from_z[z] = value
+    over_z = [send(piece, from_z.at[z], peer) for peer in z_peers]
+    for copy in over_z:
+        copy.wait()
+    piece[...] = (from_z[0] + from_z[1]) + (from_z[2] + from_z[3])
+    total_ref[core, x, y] = piece[...]
+    back_y = [send(piece, total_ref.at[core, x, y], peer) for peer in y_peers]
+    for copy in back_y:
+        copy.wait()
+    back_x = [send(total_ref.at[core, x], total_ref.at[core, x], peer) for peer in x_peers]
+    for copy in back_x:
+        copy.wait()
+    send(total_ref.at[core], total_ref.at[core], core_peer).wait()
+
+
+def sum_all(part, fit):
+    rows = part.shape[3]
+    fit_rows = fit.shape[2]
+    vmem = pl.BlockSpec(memory_space=pltpu.VMEM)
+    return pl.pallas_call(
+        exchange,
+        in_specs=[vmem, vmem],
+        out_specs=[vmem, vmem],
+        out_shape=[jax.ShapeDtypeStruct(part.shape, f32), jax.ShapeDtypeStruct((fit_rows, 128), f32)],
+        scratch_shapes=[
+            pltpu.VMEM((4, 4, rows, 128), f32),
+            pltpu.VMEM((4, 4, rows, 128), f32),
+            pltpu.VMEM((3, 4, rows, 128), f32),
+            pltpu.VMEM((4, rows, 128), f32),
+            pltpu.VMEM((3, rows, 128), f32),
+            pltpu.VMEM((rows, 128), f32),
+            pltpu.VMEM((4, rows, 128), f32),
+            pltpu.VMEM((3, 2, fit_rows, 128), f32),
+            pltpu.VMEM((2, fit_rows, 128), f32),
+            pltpu.VMEM((fit_rows, 128), f32),
+            pltpu.SemaphoreType.DMA((21,)),
+            pltpu.SemaphoreType.DMA((21,)),
+        ],
+        compiler_params=pltpu.CompilerParams(collective_id=0, has_side_effects=True),
+    )(part, fit)
 
 
 def on_device(
@@ -154,7 +251,8 @@
     degrees = jnp.sum(chosen[:, :, None] * degree[None], axis=1).reshape(sensor_rows)
     pulls = jnp.sum(chosen[:, :, None, None] * pulled[None], axis=1).reshape(sensor_rows, rank_one)
     fit_part = fit / math.sqrt(total_time * total_chan) + lap_weight * (degrees[:, None] * sensor_factor - pulls)
-    sensor_grad = lax.psum_scatter(fit_part, ("channel", "tm"), scatter_dimension=0, tiled=True)
+    fit_pack = fit_part.reshape(n_channel, n_time, 2, share // 2, rank_one)
+    fit_pack = jnp.concatenate([fit_pack[:, :, 0], fit_pack[:, :, 1]], axis=-1)
 
     inner = jnp.einsum("rkj,js->rks", folded3, channel_factor, precision=high)
     core_part = jnp.einsum("rks,kt->rts", inner, time_factor, precision=high)
@@ -162,23 +260,28 @@
     time_part = jnp.einsum("rks,rst->tk", inner, core, precision=high)
     chan_slots = jnp.where((jnp.arange(n_channel) == chan_index)[:, None, None], chan_part[None], 0.0)
     time_slots = jnp.where((jnp.arange(n_time) == time_index)[:, None, None], time_part[None], 0.0)
-    packed = jnp.concatenate(
-        [core_part.reshape(-1, 128), chan_slots.reshape(-1, 128), time_slots.reshape(-1, 128)], axis=0
-    )
-    total = lax.psum(packed, AXES)
     n_core = core_part.size // 128
     n_chan = n_channel * chan_part.size // 128
+    n_rows = n_core + n_chan + n_time * time_part.size // 128
+    piece_rows = -(-n_rows // 256) * 8
+    packed = jnp.concatenate(
+        [
+            (core_part / math.sqrt(total_sensors * total_time * total_chan)).reshape(-1, 128),
+            (chan_slots / math.sqrt(total_sensors * total_time)).reshape(-1, 128),
+            (time_slots / math.sqrt(total_sensors * total_chan)).reshape(-1, 128),
+            jnp.zeros((32 * piece_rows - n_rows, 128), f32),
+        ],
+        axis=0,
+    ).reshape(2, 4, 4, piece_rows, 128)
+    total, fit_share = sum_all(packed, fit_pack)
+    sensor_grad = jnp.concatenate([fit_share[:, :rank_one], fit_share[:, rank_one:]], axis=0)
+    total = total.reshape(-1, 128)
     core_grad = total[:n_core].reshape(rank_one, rank_three, rank_two).transpose(0, 2, 1)
     chan_all = total[n_core : n_core + n_chan].reshape(n_channel, rank_two, chan_rows)
-    time_all = total[n_core + n_chan :].reshape(n_time, rank_three, time_rows)
+    time_all = total[n_core + n_chan : n_rows].reshape(n_time, rank_three, time_rows)
     channel_grad = lax.dynamic_index_in_dim(chan_all, chan_index, 0, keepdims=False).T
     time_grad = lax.dynamic_index_in_dim(time_all, time_index, 0, keepdims=False).T
-    return (
-        core_grad / math.sqrt(total_sensors * total_time * total_chan),
-        sensor_grad,
-        channel_grad / math.sqrt(total_sensors * total_time),
-        time_grad / math.sqrt(total_sensors * total_chan),
-    )
+    return (core_grad, sensor_grad, channel_grad, time_grad)
 
 
 def solution(mesh):

time: 220 us -> 127 us (0.58)
  waiting for transfers between devices: 137 us -> 0.02 us
  Pallas kernels: 18.7 us -> 55.7 us
  local copies, waits for them, and re-layouts: 13.9 us -> 25.7 us
    psum x1 -> x0, waiting for transfers between devices: 137 us -> none  [on_device(): total = lax.psum(packed, AXES)]
    pallas_call x0 -> x1, Pallas kernels: none -> 37 us  [sum_all(): pl.pallas_call(exchange, in_specs=[vmem, vmem], out_specs=[vmem, vmem], o...]
    unnamed x21 -> x29, local copies, waits for them, and re-layouts: 2.12 us -> 6.12 us
    concatenate x1, other arithmetic: 5 us -> 2.6 us  [on_device(): jnp.concatenate([core_time, core_time], axis=2)]
  transfers between devices with their start and end apart: 3 -> 1, of which waited for: 1 -> 0; matrix products, arithmetic and copies ran while one was open for 17% -> 29% of each run, Pallas kernels for 9% -> 15%
where the time goes in v2:
time: 127 us; the launch traced here: 126 us
  Pallas kernels  55.7 us (44%)
  local copies, waits for them, and re-layouts  25.7 us (20%)
  between operations  19.9 us (16%)
  matrix products  12.4 us (10%)
  other arithmetic  12.1 us (10%)
    pallas_call x1, Pallas kernels, sum_all(): pl.pallas_call(exchange, in_specs=[vmem, vmem], out_specs=[vmem, vmem], o...  37 us
    pallas_call x1, Pallas kernels, big_pass(): pl.pallas_call(functools.partial(slab, steps), grid=(steps,), in_specs=[p...  18.7 us
    unnamed x29, local copies, waits for them, and re-layouts  6.12 us
    concatenate x1, local copies, waits for them, and re-layouts, on_device(): jnp.concatenate([core_time, core_time], axis=2)  4.51 us
    dot_general x1, matrix products, on_device(): chan_part = jnp.einsum('rkj,skr->sj', folded3, core_time, precision=high)  3.47 us
    dot_general x1, matrix products, on_device(): core_part = jnp.einsum('rks,kt->rts', inner, time_factor, precision=high)  3.17 us
    concatenate x1, other arithmetic, on_device(): jnp.concatenate([core_time, core_time], axis=2)  2.6 us
    dot_general x1, matrix products, on_device(): core_time = jnp.einsum('rst,kt->skr', core, time_factor, precision=highest)  2.56 us
  transfers between devices with their start and end apart: 1, of which 0 were waited for; matrix products, arithmetic and copies ran while one was open for 29% of the time, Pallas kernels for 15%

profile of v2, /device:TPU:1, one launch (start us, length us, event | category | flops | bytes accessed | tf_op | source)
XLA Modules:
  0.0 125.8 jit_solution(11698876559390007723)
XLA Ops:
  7.2 0.0 copy-start
  7.2 0.0 all-gather.2.cloned.1.call-start
  7.2 1.0 reshape.130
  8.3 0.7 copy.44
  9.0 0.0 all-gather.2.cloned.1.call-update
  9.0 0.5 iota_compare_fusion.1
  9.5 0.8 copy.45
  10.3 0.1 reshape.131
  10.4 0.1 dynamic_slice.25
  10.4 0.6 fusion.21
  14.8 1.9 %copy.43 = f32[768,64]{1,0:T(8,128)} copy(f32[768,64]{0,1:T(8,128)} %param.9) | data formatting | bytes 393216 | tf_op args[2]
  16.6 0.0 copy-done
  16.6 2.6 %convolution_bitcast_fusion = f32[64,64,64]{0,1,2:T(8,128)S(1)} fusion(f32[64,64,32]{1,2,0:T(8,128)S(1)} %copy-done, f32[64,32]{0,1:T(8,128)} %param.11), kind=kOutput, calls=%fused_computation.5 | convolution fusion | flops 100663296 | bytes 1581056 | tf_op jit(solution)/shard_map/rst,kt->skr/dot_general | solution.py:236
  19.2 0.0 copy-start.3
  19.2 1.4 %copy-done.3 = f32[64,64,64]{0,1,2:T(8,128)} copy-done((f32[64,64,64]{0,1,2:T(8,128)}, f32[64,64,64]{0,1,2:T(8,128)S(1)}, u32[]{:S(2)}) %copy-start.3) | copy-done | bytes 1048600
  20.6 2.6 %pad_maximum_fusion = f32[64,64,128]{0,1,2:T(8,128)} fusion(f32[64,64,64]{0,1,2:T(8,128)S(1)} %convolution_bitcast_fusion), kind=kLoop, calls=%fused_computation | loop fusion | flops 524288 | bytes 3145728 | tf_op jit(solution)/shard_map/concatenate | solution.py:237
  23.2 4.5 %copy.40 = f32[64,64,128]{2,1,0:T(8,128)S(1)} copy(f32[64,64,128]{0,1,2:T(8,128)} %pad_maximum_fusion) | data formatting | bytes 4194304 | tf_op jit(solution)/shard_map/concatenate | solution.py:237
  27.7 1.2 reduce-precision_convert_fusion
  28.9 0.0 copy-start.1
  28.9 0.0 copy-start.2
  29.0 1.9 %pad_maximum_fusion.1.ct_ref = bf16[192,8192]{1,0:T(8,128)(2,1)} fusion(bf16[64,8192]{1,0:T(8,128)(2,1)S(1)} %get-tuple-element.32, bf16[64,8192]{1,0:T(8,128)(2,1)S(1)} %get-tuple-element.31), kind=kLoop, calls=%fused_computation.1 | loop fusion | flops 9437184 | bytes 5242880 | tf_op jit(solution)/shard_map/concatenate | solution.py:239
  30.9 0.0 copy-done.1
  30.9 0.0 copy-done.2
  30.9 18.7 %shard_map.102 = (f32[64,64,128]{2,1,0:T(8,128)S(1)}, f32[768,64]{1,0:T(8,128)S(1)}) custom-call(f32[768,64,128]{2,1,0:T(8,128)} %tensor_ref.1, f32[64,768]{1,0:T(8,128)S(1)} %bitcast.69, f32[64,128]{1,0:T(8,128)S(1)} %bitcast.70, bf16[192,8192]{1,0:T(8,128)(2,1)} %pad_maximum_fusion.1.ct_ref), custom_call_target="tpu_custom_call" | custom-call | flops 8000000000 | bytes 33554432 | tf_op jit(solution)/shard_map/pallas_call | solution.py:89
  49.6 1.0 fusion.13
  50.6 0.0 copy-start.4
  50.6 1.3 %copy-done.4 = f32[64,64,64]{2,1,0:T(8,128)} copy-done((f32[64,64,64]{2,1,0:T(8,128)}, f32[64,64,64]{2,1,0:T(8,128)S(1)}, u32[]{:S(2)}) %copy-start.4) | copy-done | bytes 1048600
  51.9 1.0 convolution_bitcast_fusion.2
  52.9 0.0 copy-done.11
  52.9 0.7 select_multiply_fusion
  53.6 1.4 %div.47 = f32[32,128]{1,0:T(8,128)} reshape(f32[2,32,64]{2,1,0:T(8,128)} %select_multiply_fusion) | data formatting | bytes 32768 | tf_op jit(solution)/shard_map/div | solution.py:271
  55.0 0.6 broadcast_in_dim.59
  55.6 1.3 %broadcast_in_dim.60 = pred[256]{0:T(512)(128)(4,1)} reshape(pred[4,64]{1,0:T(4,128)(4,1)} %broadcast_in_dim.59) | data formatting | bytes 512 | tf_op jit(solution)/shard_map/jit(_where)/broadcast_in_dim | solution.py:261
  56.9 0.0 copy-done.7
  56.9 3.2 %fusion.1 = f32[64,32,64]{2,1,0:T(8,128)} fusion(f32[64,64,64]{2,1,0:T(8,128)} %copy-done.4, f32[64,32]{0,1:T(8,128)S(1)} %copy-done.7), kind=kOutput, calls=%fused_computation.7 | convolution fusion | flops 50462720 | bytes 1581056 | tf_op jit(solution)/shard_map/rks,kt->rts/dot_general | solution.py:258
  60.1 2.2 %reshape.127 = f32[1024,128]{1,0:T(8,128)} reshape(f32[64,32,64]{2,1,0:T(8,128)} %fusion.1) | data formatting | bytes 1048576 | tf_op jit(solution)/shard_map/reshape | solution.py:269
  62.3 0.0 copy-start.9
  62.3 0.7 copy.42
  63.0 0.0 copy-done.9
  63.0 3.5 %convolution_bitcast_fusion.1 = f32[64,128]{1,0:T(8,128)S(1)} fusion(f32[64,64,64]{0,1,2:T(8,128)} %copy-done.3, f32[64,64,128]{2,1,0:T(8,128)S(1)} %get-tuple-element.8), kind=kOutput, calls=%fused_computation.8 | convolution fusion | flops 201326592 | bytes 3178496 | tf_op jit(solution)/shard_map/rkj,skr->sj/dot_general | solution.py:259
  66.5 0.0 copy-done.12
  66.5 0.0 copy-start.10
  66.5 0.1 fusion.7
  66.6 0.1 pad.10.clone
  68.6 1.1 convert_reduce_fusion
  69.7 0.8 multiply_reduce_fusion.1
  70.4 2.2 %maximum_maximum_fusion = f32[1536,128]{1,0:T(8,128)} fusion(f32[32,128]{1,0:T(8,128)S(1)} %copy-done.8, f32[256,128]{1,0:T(8,128)S(1)} %fusion.7, f32[1024,128]{1,0:T(8,128)} %reshape.127, f32[1536]{0:T(1024)S(1)} %pad.10.clone), kind=kLoop, calls=%fused_computation.10 | loop fusion | flops 589824 | bytes 1464320 | tf_op jit(solution)/shard_map/concatenate | solution.py:267
  72.6 0.8 constant_dynamic-slice_fusion.2
  73.4 1.2 fusion.4
  74.6 0.0 copy-done.10
  74.6 0.1 multiply_reduce_fusion
  74.8 0.2 copy.46
  74.9 0.2 fusion.3
  75.2 0.8 pad_maximum_fusion.2.fit_ref
  76.0 37.0 %shard_map.103 = (f32[2,4,4,48,128]{4,3,2,1,0:T(8,128)}, f32[48,128]{1,0:T(8,128)}) custom-call(f32[2,4,4,48,128]{4,3,2,1,0:T(8,128)} %bitcast.72, f32[4,2,48,128]{3,2,1,0:T(8,128)} %pad_maximum_fusion.2.fit_ref), custom_call_target="tpu_custom_call" | custom-call | tf_op jit(solution)/shard_map/pallas_call | solution.py:190
  113.0 1.1 slice.42
  114.0 0.9 slice.43
  115.0 0.7 slice.44
  115.7 1.2 reshape.135
  116.9 0.1 fusion.20
  116.9 0.7 copy.50
  117.6 0.1 reshape.137
  117.7 0.6 dynamic-slice_bitcast_fusion
  118.3 0.6 dynamic-slice_bitcast_fusion.1
  (16 shorter events, 0.1 us)
Async XLA Ops:
  7.2 9.5 %copy-start = (f32[64,64,32]{1,2,0:T(8,128)S(1)}, f32[64,64,32]{1,2,0:T(8,128)}, u32[]{:S(2)}) copy-start(f32[64,64,32]{1,2,0:T(8,128)} %param.8) | copy-start | bytes 1572868
  7.2 65.4 %all-gather.2.cloned.1.call-start = ((), (), s32[]{:S(2)}) async-start(), calls=%async_computation | async-start | bytes 3342336 | tf_op jit(solution)/shard_map/all_gather | solution.py:234
  19.2 1.4 %copy-start.3 = (f32[64,64,64]{0,1,2:T(8,128)}, f32[64,64,64]{0,1,2:T(8,128)S(1)}, u32[]{:S(2)}) copy-start(f32[64,64,64]{0,1,2:T(8,128)S(1)} %convolution_bitcast_fusion) | copy-start | bytes 3145732
  28.9 1.9 %copy-start.1 = (f32[768,64]{0,1:T(8,128)S(1)}, f32[768,64]{0,1:T(8,128)}, u32[]{:S(2)}) copy-start(f32[768,64]{0,1:T(8,128)} %param.9) | copy-start | bytes 589828
  28.9 1.9 %copy-start.2 = (f32[128,64]{0,1:T(8,128)S(1)}, f32[128,64]{0,1:T(8,128)}, u32[]{:S(2)}) copy-start(f32[128,64]{0,1:T(8,128)} %param.10) | copy-start | bytes 98308
  50.6 1.3 %copy-start.4 = (f32[64,64,64]{2,1,0:T(8,128)}, f32[64,64,64]{2,1,0:T(8,128)S(1)}, u32[]{:S(2)}) copy-start(f32[64,64,64]{2,1,0:T(8,128)S(1)} %fusion.13) | copy-start | bytes 3145732
  51.9 1.0 copy-start.11
  51.9 5.0 %copy-start.7 = (f32[64,32]{0,1:T(8,128)S(1)}, f32[64,32]{0,1:T(8,128)}, u32[]{:S(2)}) copy-start(f32[64,32]{0,1:T(8,128)} %param.11) | copy-start | bytes 24580
  62.3 0.7 copy-start.9
  63.0 3.5 %copy-start.12 = (pred[256]{0:T(512)(128)(4,1)S(1)}, pred[256]{0:T(512)(128)(4,1)}, u32[]{:S(2)}) copy-start(pred[256]{0:T(512)(128)(4,1)} %broadcast_in_dim.60) | copy-start | bytes 772
  63.0 7.4 %copy-start.8 = (f32[32,128]{1,0:T(8,128)S(1)}, f32[32,128]{1,0:T(8,128)}, u32[]{:S(2)}) copy-start(f32[32,128]{1,0:T(8,128)} %div.47) | copy-start | bytes 49156
  66.5 8.2 %copy-start.10 = (f32[6,3]{1,0:T(8,128)S(1)}, f32[6,3]{1,0:T(8,128)}, u32[]{:S(2)}) copy-start(f32[6,3]{1,0:T(8,128)} %copy-done.9) | copy-start | bytes 220
  66.5 8.4 %copy-start.5 = (f32[768,64]{1,0:T(8,128)S(1)}, f32[768,64]{1,0:T(8,128)}, u32[]{:S(2)}) copy-start(f32[768,64]{1,0:T(8,128)} %copy.43) | copy-start | bytes 589828
  112.9 3.9 %copy-start.6 = (f32[48,128]{1,0:T(8,128)S(1)}, f32[48,128]{1,0:T(8,128)}, u32[]{:S(2)}) copy-start(f32[48,128]{1,0:T(8,128)} %get-tuple-element.11) | copy-start | bytes 73732
Sparse Core Ops, SparseCore 0:
  9.7 39.3 all-gather.1

commit v3 on v2

--- a/solution.py
+++ b/solution.py
@@ -20,7 +20,7 @@
     return top, (value - top.astype(f32)).astype(bf16)
 
 
-def slab(steps, tensor_ref, rows_ref, chan_ref, ct_ref, folded_ref, fit_ref, fold_lhs, chan_lhs, square_lhs, fit_sum, gram):
+def slab(steps, tensor_ref, rows_ref, chan_ref, ct_ref, inner_ref, by_chan_ref, fit_ref, fold_lhs, chan_lhs, chan_rhs, square_lhs, fit_sum, gram, by_chan):
     step = pl.program_id(0)
     sensors, slab_steps, chans = tensor_ref.shape
     rank = rows_ref.shape[0]
@@ -38,11 +38,17 @@
         square_lhs[...] = jnp.concatenate([top, top, low, jnp.zeros_like(low)], axis=1)
         top, low = split(chan_ref[...].T)
         chan_lhs[...] = jnp.concatenate([top, low, top], axis=1)
+        chan_rhs[...] = jnp.concatenate(
+            [jnp.concatenate([top, low], axis=1), jnp.concatenate([top, jnp.zeros_like(low)], axis=1)], axis=0
+        )
+        by_chan[...] = jnp.zeros_like(by_chan)
         fit_sum[...] = jnp.zeros_like(fit_sum)
         gram[...] = jnp.zeros_like(gram)
 
     flat = tensor_ref.reshape(sensors * slab_steps, chans)
-    model = jnp.dot(chan_lhs[...], ct_ref[...], preferred_element_type=f32)
+    ct_top, ct_low = split(ct_ref[...])
+    model = jnp.dot(chan_lhs[...], jnp.concatenate([ct_top, ct_top, ct_low], axis=0), preferred_element_type=f32)
+    stacked, across = [], []
     lower_half = lax.broadcasted_iota(jnp.int32, (chans, 2 * rank), 1) < rank
     for pair in range(slab_steps // 2):
         wide, narrow = [], []
@@ -62,15 +68,30 @@
             square_lhs[...], jnp.concatenate([both, first], axis=1), (((1,), (1,)), ((), ())), preferred_element_type=f32
         )
         total = own - (part[:rank] + part[rank:])
-        folded_ref[:, 2 * pair, :] = total[:, :chans]
-        folded_ref[:, 2 * pair + 1, :] = total[:, chans:]
+        total_top, total_low = split(total)
+        for k in (0, 1):
+            cut = slice(k * chans, (k + 1) * chans)
+            stacked += [total_top[:, cut], total_low[:, cut]]
+            across.append(jnp.concatenate([total_top[:, cut], total_low[:, cut]], axis=1))
         fit_sum[...] += jnp.dot(
             jnp.concatenate([top, low], axis=1), jnp.concatenate([both, first], axis=0), preferred_element_type=f32
         )
         gram[...] += lax.dot_general(both, both, (((0,), (0,)), ((), ())), preferred_element_type=f32)
 
+    by_chan[...] += jnp.dot(
+        jnp.concatenate([ct_top, ct_low], axis=0), jnp.concatenate(stacked, axis=0), preferred_element_type=f32
+    )
+    inner = jnp.dot(jnp.concatenate(across, axis=0), chan_rhs[...], preferred_element_type=f32)
+    rank_two = inner.shape[1] // 2
+    inner = inner[:, :rank_two] + inner[:, rank_two:]
+    for k in range(slab_steps):
+        upper = inner[k * rank : k * rank + rank // 2]
+        inner_ref[k] = jnp.concatenate([upper, inner[k * rank + rank // 2 : (k + 1) * rank]], axis=1)
+
     @pl.when(step == steps - 1)
     def _():
+        chan_sums = by_chan[...]
+        by_chan_ref[...] = chan_sums[:rank_two] + chan_sums[rank_two:]
         grams = gram[...]
         left = grams[:rank] + grams[rank:]
         square = left[:, :rank] + left[:, rank:]
@@ -93,19 +114,26 @@
             pl.BlockSpec((sensors, slab_steps, chans), lambda i: (0, i, 0)),
             pl.BlockSpec((rank, sensors), lambda i: (0, 0)),
             pl.BlockSpec((rank_two, chans), lambda i: (0, 0)),
-            pl.BlockSpec((3 * rank_two, slab_steps * 2 * rank), lambda i: (0, i)),
+            pl.BlockSpec((rank_two, slab_steps * 2 * rank), lambda i: (0, i)),
         ],
         out_specs=[
-            pl.BlockSpec((rank, slab_steps, chans), lambda i: (0, i, 0)),
+            pl.BlockSpec((slab_steps, rank // 2, 2 * rank_two), lambda i: (i, 0, 0)),
+            pl.BlockSpec((rank_two, chans), lambda i: (0, 0)),
             pl.BlockSpec((sensors, rank), lambda i: (0, 0)),
         ],
-        out_shape=[jax.ShapeDtypeStruct((rank, times, chans), f32), jax.ShapeDtypeStruct((sensors, rank), f32)],
+        out_shape=[
+            jax.ShapeDtypeStruct((times, rank // 2, 2 * rank_two), f32),
+            jax.ShapeDtypeStruct((rank_two, chans), f32),
+            jax.ShapeDtypeStruct((sensors, rank), f32),
+        ],
         scratch_shapes=[
             pltpu.VMEM((2 * rank, 2 * sensors), bf16),
             pltpu.VMEM((chans, 3 * rank_two), bf16),
+            pltpu.VMEM((2 * chans, 2 * rank_two), bf16),
             pltpu.VMEM((rank, 4 * rank), bf16),
             pltpu.VMEM((sensors, 2 * rank), f32),
             pltpu.VMEM((2 * rank, 2 * rank), f32),
+            pltpu.VMEM((2 * rank_two, chans), f32),
         ],
         compiler_params=pltpu.CompilerParams(vmem_limit_bytes=50 * 2**20),
         cost_estimate=pl.CostEstimate(flops=8 * 10**9, bytes_accessed=32 * 2**20, transcendentals=0),
@@ -233,11 +261,11 @@
     block_rows = rows.reshape(rank_one, blocks, block).transpose(1, 0, 2)
     whole_rows = lax.all_gather(block_rows, "sensor", axis=0, tiled=True)
 
-    core_time = jnp.einsum("rst,kt->skr", core, time_factor, precision=highest)
-    twice = jnp.concatenate([core_time, core_time], axis=2).reshape(rank_two, time_rows * 2 * rank_one)
-    top = lax.reduce_precision(twice, 8, 7)
-    ct = jnp.concatenate([top, top, twice - top], axis=0).astype(bf16)
-    folded3, fit = big_pass(tensor, rows, channel_factor.T, ct)
+    by_rank = core.transpose(1, 2, 0)
+    twice = jnp.einsum("kt,str->skr", time_factor, jnp.concatenate([by_rank, by_rank], axis=2), precision=highest)
+    inner, chan_part, fit = big_pass(
+        tensor, rows, channel_factor.T, twice.reshape(rank_two, time_rows * 2 * rank_one)
+    )
 
     pairs = blocks * slots // groups
     first = share_index * pairs
@@ -254,10 +282,9 @@
     fit_pack = fit_part.reshape(n_channel, n_time, 2, share // 2, rank_one)
     fit_pack = jnp.concatenate([fit_pack[:, :, 0], fit_pack[:, :, 1]], axis=-1)
 
-    inner = jnp.einsum("rkj,js->rks", folded3, channel_factor, precision=high)
-    core_part = jnp.einsum("rks,kt->rts", inner, time_factor, precision=high)
-    chan_part = jnp.einsum("rkj,skr->sj", folded3, core_time, precision=high)
-    time_part = jnp.einsum("rks,rst->tk", inner, core, precision=high)
+    halves = core.reshape(2, rank_one // 2, rank_two, rank_three).transpose(3, 1, 0, 2).reshape(rank_three, rank_one // 2, 2 * rank_two)
+    core_part = jnp.einsum("kt,kam->tam", time_factor, inner, precision=high)
+    time_part = jnp.einsum("kam,tam->tk", inner, halves, precision=high)
     chan_slots = jnp.where((jnp.arange(n_channel) == chan_index)[:, None, None], chan_part[None], 0.0)
     time_slots = jnp.where((jnp.arange(n_time) == time_index)[:, None, None], time_part[None], 0.0)
     n_core = core_part.size // 128
@@ -276,7 +303,8 @@
     total, fit_share = sum_all(packed, fit_pack)
     sensor_grad = jnp.concatenate([fit_share[:, :rank_one], fit_share[:, rank_one:]], axis=0)
     total = total.reshape(-1, 128)
-    core_grad = total[:n_core].reshape(rank_one, rank_three, rank_two).transpose(0, 2, 1)
+    core_sum = total[:n_core].reshape(rank_three, rank_one // 2, 2, rank_two)
+    core_grad = core_sum.transpose(2, 1, 3, 0).reshape(rank_one, rank_two, rank_three)
     chan_all = total[n_core : n_core + n_chan].reshape(n_channel, rank_two, chan_rows)
     time_all = total[n_core + n_chan : n_rows].reshape(n_time, rank_three, time_rows)
     channel_grad = lax.dynamic_index_in_dim(chan_all, chan_index, 0, keepdims=False).T

time: 127 us -> 109 us (0.86)
  other arithmetic: 12.1 us -> 3.6 us
  matrix products: 12.4 us -> 5.23 us
  local copies, waits for them, and re-layouts: 25.7 us -> 22.1 us
  Pallas kernels: 55.7 us -> 57.5 us
    dot_general x5 -> x3, matrix products: 11.2 us -> 3.99 us  [the longest x1 1.93 us: on_device(): jnp.einsum('kt,str->skr', time_factor, jnp.concatenate([by_rank, by_rank]...]
    concatenate x1 -> x0, local copies, waits for them, and re-layouts: 4.51 us -> none  [on_device(): jnp.concatenate([core_time, core_time], axis=2)]
    concatenate x2 -> x0, other arithmetic: 4.5 us -> none  [the longest x1 2.6 us: on_device(): jnp.concatenate([core_time, core_time], axis=2)]
    pallas_call x1, Pallas kernels: 18.7 us -> 20.5 us  [big_pass(): pl.pallas_call(functools.partial(slab, steps), grid=(steps,), in_specs=[p...]
    transpose x0 -> x1, local copies, waits for them, and re-layouts: none -> 1.79 us  [on_device(): core.reshape(2, rank_one // 2, rank_two, rank_three).transpose(3, 1, 0, 2)]
    broadcast_in_dim x2, local copies, waits for them, and re-layouts: 1.86 us -> 0.16 us  [on_device(): jnp.where((jnp.arange(n_channel) == chan_index)[:, None, None], chan_part...]
    reshape x2 -> x3, local copies, waits for them, and re-layouts: 3.4 us -> 4.81 us  [the longest x1 2.63 us: on_device(): core.reshape(2, rank_one // 2, rank_two, rank_three).transpose(3, 1, 0, 2)]
    div x1, local copies, waits for them, and re-layouts: 1.43 us -> 0.08 us  [on_device(): time_slots / math.sqrt(total_sensors * total_chan)]
  transfers between devices with their start and end apart: 1 -> 1, of which waited for: 0 -> 0; matrix products, arithmetic and copies ran while one was open for 29% -> 16% of each run, Pallas kernels for 15% -> 19%
where the time goes in v3:
time: 109 us
  Pallas kernels  57.5 us (53%)
  local copies, waits for them, and re-layouts  22.1 us (20%)
  between operations  20.1 us (18%)
  matrix products  5.23 us (5%)
  other arithmetic  3.6 us (3%)
    pallas_call x1, Pallas kernels, sum_all(): pl.pallas_call(exchange, in_specs=[vmem, vmem], out_specs=[vmem, vmem], o...  37 us
    pallas_call x1, Pallas kernels, big_pass(): pl.pallas_call(functools.partial(slab, steps), grid=(steps,), in_specs=[p...  20.5 us
    unnamed x23, local copies, waits for them, and re-layouts  6.38 us
    reshape x1, local copies, waits for them, and re-layouts, on_device(): core.reshape(2, rank_one // 2, rank_two, rank_three).transpose(3, 1, 0, 2)  2.63 us
    reshape x2, local copies, waits for them, and re-layouts, on_device(): core_sum = total[:n_core].reshape(rank_three, rank_one // 2, 2, rank_two)  2.19 us
  transfers between devices with their start and end apart: 1, of which 0 were waited for; matrix products, arithmetic and copies ran while one was open for 16% of the time, Pallas kernels for 19%

profile of v3, /device:TPU:1, one launch (start us, length us, event | category | flops | bytes accessed | tf_op | source)
XLA Modules:
  0.0 108.6 jit_solution(8457098878419277158)
XLA Ops:
  7.2 0.0 copy-start
  7.2 0.0 copy-start.5
  7.2 0.0 all-gather.2.cloned.1.call-start
  7.2 1.0 reshape.141
  8.3 0.7 copy.56
  9.0 0.0 all-gather.2.cloned.1.call-update
  9.0 0.8 copy.57
  9.8 0.1 reshape.142
  9.9 0.1 dynamic_slice.25
  10.0 0.6 fusion.25
  14.5 1.9 %copy.55 = f32[768,64]{1,0:T(8,128)} copy(f32[768,64]{0,1:T(8,128)} %param.9) | data formatting | bytes 393216 | tf_op args[2]
  16.3 0.1 copy.54
  16.4 0.0 copy-done.5
  16.4 1.1 copy.49
  17.5 0.0 copy-done
  17.5 1.9 %fusion.1 = f32[64,128,64]{1,2,0:T(8,128)S(1)} fusion(f32[64,32,64]{2,1,0:T(8,128)S(1)} %bitcast.70, f32[64,32]{0,1:T(8,128)S(1)} %copy-done), kind=kOutput, calls=%fused_computation.4 | convolution fusion | flops 201588736 | bytes 2629632 | tf_op jit(solution)/shard_map/kt,str->skr/dot_general | solution.py:265
  19.5 0.0 copy-start.6
  19.5 1.2 %copy.75 = f32[8,8,64,128]{3,1,2,0:T(8,128)S(1)} copy(f32[8,8,64,128]{3,2,1,0:T(8,128)S(1)} %bitcast.69) | data formatting | bytes 4194304
  20.7 0.0 copy-start.1
  20.7 0.0 copy-start.4
  20.7 0.0 copy-done.6
  20.7 1.8 %copy.52 = f32[32,32,2,64]{3,2,0,1:T(2,128)} copy(f32[32,32,2,64]{3,0,1,2:T(8,128)S(1)} %bitcast.71) | data formatting | bytes 1048576 | tf_op jit(solution)/shard_map/transpose | solution.py:285
  22.5 2.6 %reshape.138 = f32[32,32,128]{2,0,1:T(8,128)} reshape(f32[32,32,2,64]{3,2,0,1:T(2,128)} %copy.52) | data formatting | bytes 1048576 | tf_op jit(solution)/shard_map/reshape | solution.py:285
  25.1 0.0 copy-done.1
  25.1 0.0 copy-done.4
  25.1 0.0 copy-start.7
  25.1 20.5 %shard_map.102 = (f32[64,32,128]{2,1,0:T(8,128)S(1)}, f32[64,128]{1,0:T(8,128)S(1)}, f32[768,64]{1,0:T(8,128)S(1)}) custom-call(f32[768,64,128]{2,1,0:T(8,128)} %tensor_ref.1, f32[64,768]{1,0:T(8,128)S(1)} %bitcast.67, f32[64,128]{1,0:T(8,128)S(1)} %bitcast.68, f32[64,8192]{1,0:T(8,128)S(1)} %bitcast.65), custom_call_target="tpu_custom_call" | custom-call | flops 8000000000 | bytes 33554432 | tf_op jit(solution)/shard_map/pallas_call | solution.py:110
  45.7 0.0 copy-start.2
  45.7 0.7 copy-done.2
  46.4 0.0 copy-done.7
  46.4 1.1 convolution_bitcast_fusion
  47.5 0.1 select_multiply_fusion
  47.6 0.1 div.47
  47.7 0.1 broadcast_in_dim.59
  47.8 0.1 broadcast_in_dim.60
  47.9 1.0 fusion
  48.8 0.0 copy-start.3
  48.9 0.0 copy-start.8
  48.9 0.3 copy.51
  51.1 0.1 fusion.12
  51.2 0.1 pad.10.clone
  51.3 1.1 convert_reduce_fusion
  52.4 0.1 multiply_reduce_fusion.1
  52.5 1.2 %maximum_maximum_fusion = f32[1536,128]{1,0:T(8,128)} fusion(f32[32,128]{1,0:T(8,128)S(1)} %div.47, f32[256,128]{1,0:T(8,128)S(1)} %fusion.12, f32[1024,128]{1,0:T(8,128)S(1)} %bitcast.73, f32[1536]{0:T(1024)S(1)} %pad.10.clone), kind=kLoop, calls=%fused_computation.10 | loop fusion | flops 589824 | bytes 1464320 | tf_op jit(solution)/shard_map/concatenate | solution.py:294
  53.6 0.0 all-gather.2.cloned.1.call-done
  53.6 0.8 constant_dynamic-slice_fusion.2
  54.4 1.2 %fusion.9 = f32[3,128,64]{1,2,0:T(8,128)S(1)} fusion(s32[24,128,128]{2,1,0:T(8,128)} %bitcast.82, s32[]{:T(128)S(6)} %select_n.45, f32[1,64,128]{2,1,0:T(8,128)S(1)} %get-tuple-element.31, f32[1,64,128]{2,1,0:T(8,128)S(1)} %get-tuple-element.32, f32[1,64,128]{2,1,0:T(8,128)S(1)} %get-tuple-element.30), kind=kOutput, calls=%fused_computation.18 | convolution fusion | flops 18972672 | bytes 393220 | tf_op jit(solution)/shard_map/qac,qdc->qad/dot_general | solution.py:275
  55.7 0.1 multiply_reduce_fusion
  55.8 0.2 copy.58
  55.9 0.0 copy-done.3
  56.0 0.0 copy-done.8
  56.0 0.2 fusion.8
  56.2 0.8 pad_maximum_fusion.fit_ref
  57.0 37.0 %shard_map.103 = (f32[2,4,4,48,128]{4,3,2,1,0:T(8,128)}, f32[48,128]{1,0:T(8,128)}) custom-call(f32[2,4,4,48,128]{4,3,2,1,0:T(8,128)} %bitcast.72, f32[4,2,48,128]{3,2,1,0:T(8,128)} %pad_maximum_fusion.fit_ref), custom_call_target="tpu_custom_call" | custom-call | tf_op jit(solution)/shard_map/pallas_call | solution.py:218
  94.0 1.1 slice.42
  95.0 0.9 slice.43
  95.9 0.7 slice.44
  96.7 0.9 fusion.24
  97.6 0.7 copy.63
  98.3 0.6 reshape.146
  98.9 1.6 %copy.62 = f32[32,32,2,64]{3,0,1,2:T(8,128)} copy(f32[32,32,2,64]{3,2,1,0:T(2,128)S(1)} %reshape.146) | data formatting | bytes 1048576 | tf_op jit(solution)/shard_map/reshape | solution.py:306
  100.5 0.1 reshape.149
  100.5 0.6 dynamic-slice_bitcast_fusion
  101.2 0.6 dynamic-slice_bitcast_fusion.1
  (7 shorter events, 0.1 us)
Async XLA Ops:
  7.2 10.3 %copy-start = (f32[64,32]{0,1:T(8,128)S(1)}, f32[64,32]{0,1:T(8,128)}, u32[]{:S(2)}) copy-start(f32[64,32]{0,1:T(8,128)} %param.11) | copy-start | bytes 24580
  7.2 9.2 %copy-start.5 = (f32[64,64,32]{1,2,0:T(8,128)S(1)}, f32[64,64,32]{1,2,0:T(8,128)}, u32[]{:S(2)}) copy-start(f32[64,64,32]{1,2,0:T(8,128)} %param.8) | copy-start | bytes 1572868
  7.2 46.4 %all-gather.2.cloned.1.call-start = ((), (), s32[]{:S(2)}) async-start(), calls=%async_computation | async-start | bytes 3342336 | tf_op jit(solution)/shard_map/all_gather | solution.py:262
  19.5 1.2 %copy-start.6 = (f32[64,64,32]{1,2,0:T(8,128)S(1)}, f32[64,64,32]{1,2,0:T(8,128)}, u32[]{:S(2)}) copy-start(f32[64,64,32]{1,2,0:T(8,128)} %param.8) | copy-start | bytes 1572868
  20.7 4.5 %copy-start.1 = (f32[768,64]{0,1:T(8,128)S(1)}, f32[768,64]{0,1:T(8,128)}, u32[]{:S(2)}) copy-start(f32[768,64]{0,1:T(8,128)} %param.9) | copy-start | bytes 589828
  20.7 4.4 %copy-start.4 = (f32[128,64]{0,1:T(8,128)S(1)}, f32[128,64]{0,1:T(8,128)}, u32[]{:S(2)}) copy-start(f32[128,64]{0,1:T(8,128)} %param.10) | copy-start | bytes 98308
  25.1 21.3 %copy-start.7 = (f32[32,32,128]{2,0,1:T(8,128)S(1)}, f32[32,32,128]{2,0,1:T(8,128)}, u32[]{:S(2)}) copy-start(f32[32,32,128]{2,0,1:T(8,128)} %reshape.138) | copy-start | bytes 1572868
  45.7 0.7 copy-start.2
  48.8 7.1 %copy-start.3 = (f32[768,64]{1,0:T(8,128)S(1)}, f32[768,64]{1,0:T(8,128)}, u32[]{:S(2)}) copy-start(f32[768,64]{1,0:T(8,128)} %copy-done.2) | copy-start | bytes 589828
  48.9 7.1 %copy-start.8 = (f32[768,64]{1,0:T(8,128)S(1)}, f32[768,64]{1,0:T(8,128)}, u32[]{:S(2)}) copy-start(f32[768,64]{1,0:T(8,128)} %copy.55) | copy-start | bytes 589828
Sparse Core Ops, SparseCore 0:
  9.7 39.3 all-gather.1

commit v4 on v3

--- a/solution.py
+++ b/solution.py
@@ -162,7 +162,7 @@
         pl.semaphore_signal(barrier, inc=1, device_id=device(*peer), device_id_type=pl.DeviceIdType.MESH)
     pl.semaphore_wait(barrier, 10)
 
-    slot = iter(range(21))
+    slot = iter(range(27))
 
     def send(source, target, peer):
         at = next(slot)
@@ -177,11 +177,15 @@
         copy.start()
         return copy
 
-    to_core = send(part_ref.at[1 - core], from_core, core_peer)
+    order = [peer[0] for peer in x_peers] + [x]
+    to_core = [send(part_ref.at[1 - core, at], from_core.at[at], core_peer) for at in order]
     fits = [send(fit_ref.at[peer[0]], fit_x.at[d], peer) for d, peer in enumerate(x_peers)]
-    to_core.wait()
-    half[...] = part_ref[core] + from_core[...]
-    over_x = [send(half.at[peer[0]], from_x.at[d], peer) for d, peer in enumerate(x_peers)]
+    over_x = []
+    for d, at in enumerate(order):
+        to_core[d].wait()
+        half[at] = part_ref[core, at] + from_core[at]
+        if d < 3:
+            over_x.append(send(half.at[at], from_x.at[d], x_peers[d]))
     for copy in fits:
         copy.wait()
     fit_half[...] = (fit_ref[x] + fit_x[0]) + (fit_x[1] + fit_x[2])
@@ -206,9 +210,13 @@
     for copy in back_y:
         copy.wait()
     back_x = [send(total_ref.at[core, x], total_ref.at[core, x], peer) for peer in x_peers]
-    for copy in back_x:
-        copy.wait()
-    send(total_ref.at[core], total_ref.at[core], core_peer).wait()
+    across = [send(total_ref.at[core, x], total_ref.at[core, x], core_peer)]
+    for d, copy in enumerate(back_x):
+        copy.wait()
+        came = turn(x, 3 - d)
+        across.append(send(total_ref.at[core, came], total_ref.at[core, came], core_peer))
+    for copy in across:
+        copy.wait()
 
 
 def sum_all(part, fit):
@@ -231,8 +239,8 @@
             pltpu.VMEM((3, 2, fit_rows, 128), f32),
             pltpu.VMEM((2, fit_rows, 128), f32),
             pltpu.VMEM((fit_rows, 128), f32),
-            pltpu.SemaphoreType.DMA((21,)),
-            pltpu.SemaphoreType.DMA((21,)),
+            pltpu.SemaphoreType.DMA((27,)),
+            pltpu.SemaphoreType.DMA((27,)),
         ],
         compiler_params=pltpu.CompilerParams(collective_id=0, has_side_effects=True),
     )(part, fit)
@@ -282,9 +290,10 @@
     fit_pack = fit_part.reshape(n_channel, n_time, 2, share // 2, rank_one)
     fit_pack = jnp.concatenate([fit_pack[:, :, 0], fit_pack[:, :, 1]], axis=-1)
 
-    halves = core.reshape(2, rank_one // 2, rank_two, rank_three).transpose(3, 1, 0, 2).reshape(rank_three, rank_one // 2, 2 * rank_two)
     core_part = jnp.einsum("kt,kam->tam", time_factor, inner, precision=high)
-    time_part = jnp.einsum("kam,tam->tk", inner, halves, precision=high)
+    half = rank_one // 2
+    time_part = jnp.einsum("kas,ast->tk", inner[:, :, :rank_two], core[:half], precision=high)
+    time_part += jnp.einsum("kas,ast->tk", inner[:, :, rank_two:], core[half:], precision=high)
     chan_slots = jnp.where((jnp.arange(n_channel) == chan_index)[:, None, None], chan_part[None], 0.0)
     time_slots = jnp.where((jnp.arange(n_time) == time_index)[:, None, None], time_part[None], 0.0)
     n_core = core_part.size // 128

time: 109 us -> 104 us (0.954)
  local copies, waits for them, and re-layouts: 22.1 us -> 15.7 us
  matrix products: 5.23 us -> 6.48 us
    reshape x1 -> x0, local copies, waits for them, and re-layouts: 2.63 us -> none  [on_device(): core.reshape(2, rank_one // 2, rank_two, rank_three).transpose(3, 1, 0, 2)]
    transpose x1 -> x0, local copies, waits for them, and re-layouts: 1.79 us -> none  [on_device(): core.reshape(2, rank_one // 2, rank_two, rank_three).transpose(3, 1, 0, 2)]
    unnamed x23 -> x15, local copies, waits for them, and re-layouts: 6.38 us -> 4.87 us
    dot_general x1 -> x2, matrix products: 1.08 us -> 2.33 us  [the longest x1 1.17 us: on_device(): jnp.einsum('kas,ast->tk', inner[:, :, :rank_two], core[:half], precision=...]
  transfers between devices with their start and end apart: 1 -> 1, of which waited for: 0 -> 0; matrix products, arithmetic and copies ran while one was open for 16% -> 13% of each run, Pallas kernels for 19% -> 20%
where the time goes in v4:
time: 104 us; the launch traced here: 103 us
  Pallas kernels  57.2 us (55%)
  between operations  20.1 us (19%)
  local copies, waits for them, and re-layouts  15.7 us (15%)
  matrix products  6.48 us (6%)
  other arithmetic  3.61 us (3%)
    pallas_call x1, Pallas kernels, sum_all(): pl.pallas_call(exchange, in_specs=[vmem, vmem], out_specs=[vmem, vmem], o...  36.7 us
    pallas_call x1, Pallas kernels, big_pass(): pl.pallas_call(functools.partial(slab, steps), grid=(steps,), in_specs=[p...  20.5 us
    unnamed x15, local copies, waits for them, and re-layouts  4.87 us
    reshape x2, local copies, waits for them, and re-layouts, on_device(): core_sum = total[:n_core].reshape(rank_three, rank_one // 2, 2, rank_two)  2.19 us
  transfers between devices with their start and end apart: 1, of which 0 were waited for; matrix products, arithmetic and copies ran while one was open for 13% of the time, Pallas kernels for 20%

profile of v4, /device:TPU:1, one launch (start us, length us, event | category | flops | bytes accessed | tf_op | source)
XLA Modules:
  0.0 103.2 jit_solution(10192890010677139318)
XLA Ops:
  7.2 0.0 copy-start
  7.2 0.0 copy-start.3
  7.2 0.0 all-gather.2.cloned.1.call-start
  7.2 1.0 %reshape.133 = f32[64,6,128]{2,1,0:T(8,128)S(1)} reshape(f32[64,768]{1,0:T(8,128)} %bitcast.66) | data formatting | bytes 393216 | tf_op jit(solution)/shard_map/reshape | solution.py:269
  8.3 0.7 copy.56
  9.0 0.0 all-gather.2.cloned.1.call-update
  9.0 0.8 copy.57
  9.8 0.1 reshape.134
  9.9 0.1 dynamic_slice.25
  10.0 0.6 fusion.31
  14.4 1.1 %copy.55 = f32[768,64]{1,0:T(8,128)S(1)} copy(f32[768,64]{0,1:T(8,128)} %param.9) | data formatting | bytes 393216 | tf_op args[2]
  15.5 0.0 copy-done.3
  15.5 1.1 %copy.49 = f32[64,64,32]{0,2,1:T(8,128)S(1)} copy(f32[64,64,32]{1,2,0:T(8,128)S(1)} %copy-done.3) | data formatting | bytes 1048576 | tf_op args[1]
  16.6 0.0 copy-done
  16.6 1.9 %fusion.3 = f32[64,128,64]{1,2,0:T(8,128)S(1)} fusion(f32[64,32,64]{2,1,0:T(8,128)S(1)} %bitcast.70, f32[64,32]{0,1:T(8,128)S(1)} %copy-done), kind=kOutput, calls=%fused_computation.7 | convolution fusion | flops 201588736 | bytes 2629632 | tf_op jit(solution)/shard_map/kt,str->skr/dot_general | solution.py:273
  18.6 0.0 copy-start.1
  18.6 0.0 copy-start.2
  18.6 1.2 %copy.77 = f32[8,8,64,128]{3,1,2,0:T(8,128)S(1)} copy(f32[8,8,64,128]{3,2,1,0:T(8,128)S(1)} %bitcast.69) | data formatting | bytes 4194304
  19.8 0.0 copy-done.1
  19.8 0.0 copy-done.2
  19.8 20.5 %shard_map.102 = (f32[64,32,128]{2,1,0:T(8,128)S(1)}, f32[64,128]{1,0:T(8,128)S(1)}, f32[768,64]{1,0:T(8,128)S(1)}) custom-call(f32[768,64,128]{2,1,0:T(8,128)} %tensor_ref.1, f32[64,768]{1,0:T(8,128)S(1)} %bitcast.67, f32[64,128]{1,0:T(8,128)S(1)} %bitcast.68, f32[64,8192]{1,0:T(8,128)S(1)} %bitcast.65), custom_call_target="tpu_custom_call" | custom-call | flops 8000000000 | bytes 33554432 | tf_op jit(solution)/shard_map/pallas_call | solution.py:110
  40.3 0.4 fusion.29
  40.7 1.2 %convolution_bitcast_fusion = f32[64,32]{0,1:T(8,128)S(1)} fusion(f32[64,32,64]{2,1,0:T(8,128)S(1)} %get-tuple-element.34, f32[64,64,32]{1,2,0:T(8,128)S(1)} %copy-done.3), kind=kOutput, calls=%fused_computation.3 | convolution fusion | flops 25165824 | bytes 1581056 | tf_op jit(solution)/shard_map/kas,ast->tk/dot_general | solution.py:296
  41.8 1.2 %fusion.2 = f32[32,64]{1,0:T(8,128)S(1)} fusion(f32[64,32]{0,1:T(8,128)S(1)} %convolution_bitcast_fusion, f32[64,32,64]{2,1,0:T(8,128)S(1)} %get-tuple-element.33, f32[64,64,32]{1,2,0:T(8,128)S(1)} %copy-done.3), kind=kOutput, calls=%fused_computation.6 | convolution fusion | flops 25167872 | bytes 1597440 | tf_op jit(solution)/shard_map/kas,ast->tk/dot_general | solution.py:295
  43.0 0.1 select_multiply_fusion
  43.1 0.1 div.47
  43.2 0.1 broadcast_in_dim.59
  43.3 0.1 broadcast_in_dim.60
  43.3 1.0 fusion
  44.3 0.3 copy.51
  44.7 0.1 copy.54
  44.8 0.1 fusion.17
  44.9 0.1 pad.10.clone
  46.9 1.1 %convert_reduce_fusion = f32[3,128]{1,0:T(4,128)S(1)} fusion(s32[24,128,128]{2,1,0:T(8,128)} %bitcast.80, s32[]{:T(128)S(6)} %select_n.45), kind=kLoop, calls=%fused_computation.26 | loop fusion | flops 97920 | bytes 198148 | tf_op jit(solution)/shard_map/reduce_sum | solution.py:284
  48.0 0.1 multiply_reduce_fusion.1
  48.1 1.2 %maximum_maximum_fusion = f32[1536,128]{1,0:T(8,128)} fusion(f32[32,128]{1,0:T(8,128)S(1)} %div.47, f32[256,128]{1,0:T(8,128)S(1)} %fusion.17, f32[1024,128]{1,0:T(8,128)S(1)} %bitcast.72, f32[1536]{0:T(1024)S(1)} %pad.10.clone), kind=kLoop, calls=%fused_computation.14 | loop fusion | flops 589824 | bytes 1464320 | tf_op jit(solution)/shard_map/concatenate | solution.py:303
  49.2 0.0 all-gather.2.cloned.1.call-done
  49.2 0.8 constant_dynamic-slice_fusion.2
  50.0 1.2 %fusion.14 = f32[3,128,64]{1,2,0:T(8,128)S(1)} fusion(s32[24,128,128]{2,1,0:T(8,128)} %bitcast.81, s32[]{:T(128)S(6)} %select_n.45, f32[1,64,128]{2,1,0:T(8,128)S(1)} %get-tuple-element.31, f32[1,64,128]{2,1,0:T(8,128)S(1)} %get-tuple-element.32, f32[1,64,128]{2,1,0:T(8,128)S(1)} %get-tuple-element.30), kind=kOutput, calls=%fused_computation.24 | convolution fusion | flops 18972672 | bytes 393220 | tf_op jit(solution)/shard_map/qac,qdc->qad/dot_general | solution.py:283
  51.3 0.1 multiply_reduce_fusion
  51.4 0.2 copy.58
  51.5 0.2 fusion.13
  51.8 0.8 pad_maximum_fusion.fit_ref
  52.6 36.7 %shard_map.103 = (f32[2,4,4,48,128]{4,3,2,1,0:T(8,128)}, f32[48,128]{1,0:T(8,128)}) custom-call(f32[2,4,4,48,128]{4,3,2,1,0:T(8,128)} %bitcast.71, f32[4,2,48,128]{3,2,1,0:T(8,128)} %pad_maximum_fusion.fit_ref), custom_call_target="tpu_custom_call" | custom-call | tf_op jit(solution)/shard_map/pallas_call | solution.py:226
  89.3 1.1 %slice.58 = f32[1024,128]{1,0:T(8,128)S(1)} slice(f32[1536,128]{1,0:T(8,128)} %bitcast.76), slice={[0:1024], [0:128]} | slice | bytes 1048576 | tf_op jit(solution)/shard_map/slice | solution.py:315
  90.4 0.0 copy-start.4
  90.4 0.9 slice.59
  91.3 0.7 slice.60
  92.1 0.6 reshape.138
  92.7 1.6 %copy.62 = f32[32,32,2,64]{3,0,1,2:T(8,128)} copy(f32[32,32,2,64]{3,2,1,0:T(2,128)S(1)} %reshape.138) | data formatting | bytes 1048576 | tf_op jit(solution)/shard_map/reshape | solution.py:315
  94.3 0.0 copy-done.4
  94.3 0.1 fusion.30
  94.4 0.7 copy.63
  95.1 0.1 reshape.141
  95.1 0.6 dynamic-slice_bitcast_fusion
  95.7 0.6 dynamic-slice_bitcast_fusion.1
  (7 shorter events, 0.1 us)
Async XLA Ops:
  7.2 9.5 %copy-start = (f32[64,32]{0,1:T(8,128)S(1)}, f32[64,32]{0,1:T(8,128)}, u32[]{:S(2)}) copy-start(f32[64,32]{0,1:T(8,128)} %param.11) | copy-start | bytes 24580
  7.2 8.3 %copy-start.3 = (f32[64,64,32]{1,2,0:T(8,128)S(1)}, f32[64,64,32]{1,2,0:T(8,128)}, u32[]{:S(2)}) copy-start(f32[64,64,32]{1,2,0:T(8,128)} %param.8) | copy-start | bytes 1572868
  7.2 42.0 %all-gather.2.cloned.1.call-start = ((), (), s32[]{:S(2)}) async-start(), calls=%async_computation | async-start | bytes 3342336 | tf_op jit(solution)/shard_map/all_gather | solution.py:270
  18.6 1.2 %copy-start.1 = (f32[768,64]{0,1:T(8,128)S(1)}, f32[768,64]{0,1:T(8,128)}, u32[]{:S(2)}) copy-start(f32[768,64]{0,1:T(8,128)} %param.9) | copy-start | bytes 589828
  18.6 1.2 %copy-start.2 = (f32[128,64]{0,1:T(8,128)S(1)}, f32[128,64]{0,1:T(8,128)}, u32[]{:S(2)}) copy-start(f32[128,64]{0,1:T(8,128)} %param.10) | copy-start | bytes 98308
  90.4 3.9 %copy-start.4 = (f32[48,128]{1,0:T(8,128)S(1)}, f32[48,128]{1,0:T(8,128)}, u32[]{:S(2)}) copy-start(f32[48,128]{1,0:T(8,128)} %get-tuple-element.13) | copy-start | bytes 73732
Sparse Core Ops, SparseCore 0:
  9.7 39.3 all-gather.1
